TPU v7x, 32 devices: a whole 2x2x4 slice. The times are simulated.
32 devices in a mesh: row: 8 (over z, core), col: 4 (over y, x).
Axes of the slice: x: 2, y: 2, z: 4, core: 2. Of those that a mesh axis runs over, the one named last changes fastest.
Arguments:
- pivot_inverse: float32 [1024, 1024], P('row'), may hold values from -1 to 2, as said below
- panel: float32 [16, 1024, 1024], P('row', 'col'), may hold values from -1 to 1
- trailing: float32 [160, 1024, 1024], P('row', None, 'col'), may hold values from -6 to 6
- tile_list: int32 [160, 2], P('row'), may hold values from -1 to 15, as said below
Outputs:
- solved_panel: float32 [16, 1024, 1024], P('row', 'col')
- updated: float32 [160, 1024, 1024], P('row', None, 'col')
Inputs may be any that keep to these rules, and one draw needn't show every extreme that they name: `pivot_inverse`: lower triangular, diagonal between 0.5 and 2. `tile_list`: slots t of group g are g * 20 to g * 20 + 19. Column 0 lies in 0 to 1; column 1 is a panel tile or -1 for an empty slot. The live slots of a group come first and name distinct pairs; each group in the first half of the groups holds exactly 6 live slots, each in the second half exactly 20. Empty slots hold 0 in column 0.
All inputs are finite; a program needn't handle non-finite values.
Results may differ from a plain program's by a relative error of at most 0.00007.
Values sent between devices are 32-bit elements; how exact they have to be, the bound alone decides.
A program may use at most 128 MiB of HBM per device.

v0:
```python
import jax
import jax.numpy as jnp
from jax import lax
from jax.sharding import PartitionSpec as P

highest = lax.Precision.HIGHEST


def slot_term(left_tile, right_rows):
    return jnp.einsum("ak,bk->ab", left_tile, right_rows, precision=highest)


def per_device(pivot_inverse, panel, trailing, tile_list):
    full_pivot = lax.all_gather(pivot_inverse, "row", axis=0, tiled=True)
    slice_rows = panel.shape[1]
    tile_order = panel.shape[2]
    solved = jnp.einsum("pak,jk->paj", panel, full_pivot, precision=highest)
    whole_tiles = lax.all_gather(solved, "col", axis=1, tiled=True)
    slices = lax.all_gather(solved, "row", axis=0, tiled=True)
    empty_term = jnp.zeros((tile_order, slice_rows), jnp.float32)

    def owner_slot(listed):
        return lax.cond(
            listed[1] >= 0,
            lambda: slot_term(whole_tiles[listed[0]], slices[jnp.maximum(listed[1], 0)]),
            lambda: empty_term,
        )

    updates = lax.map(owner_slot, tile_list)
    return (solved, trailing - updates)


def solution(mesh):
    placed = (P("row", None), P("row", "col", None), P("row", None, "col"), P("row", None))
    return jax.shard_map(
        per_device,
        mesh=mesh,
        in_specs=placed,
        out_specs=(P("row", "col", None), P("row", None, "col")),
        check_vma=False,
    )
```

profile of v0, /device:TPU:27, one launch (start us, length us, event | category | flops | bytes accessed | tf_op | source)
XLA Modules:
  0.0 548.0 jit_solution(17229575436404876348)
XLA Ops:
  8.0 47.7 %all-gather.4.cloned.1.call-done = f32[1024,1024]{1,0:T(8,128)} async-done(((f32[128,1024]{1,0:T(8,128)}), f32[1024,1024]{1,0:T(8,128)}) %all-gather.4.cloned.1.call-update) | async-done | bytes 4194320 | tf_op jit(solution)/shard_map/all_gather | solution.py:14
  55.7 9.6 %fusion.9 = f32[2,256,1024]{2,1,0:T(8,128)} fusion(f32[2,256,1024]{2,1,0:T(8,128)S(1)} %copy-done, f32[1024,1024]{1,0:T(8,128)} %all-gather.4.cloned.1.call-done), kind=kOutput, calls=%fused_computation.9 | convolution fusion | flops 6442450944 | bytes 8388608 | tf_op jit(solution)/shard_map/pak,jk->paj/dot_general | solution.py:17
  66.2 87.2 %all-gather.6.cloned.1.call-done = f32[2,1024,1024]{2,1,0:T(8,128)} async-done(((f32[2,256,1024]{2,1,0:T(8,128)}), f32[2,1024,1024]{2,1,0:T(8,128)}) %all-gather.6.cloned.1.call-update) | async-done | bytes 8388624 | tf_op jit(solution)/shard_map/all_gather | solution.py:18
  153.4 151.0 %all-gather.8.cloned.1.call-done = f32[16,256,1024]{2,1,0:T(8,128)} async-done(((f32[2,256,1024]{2,1,0:T(8,128)}), f32[16,256,1024]{2,1,0:T(8,128)}) %all-gather.8.cloned.1.call-update) | async-done | bytes 16777232 | tf_op jit(solution)/shard_map/all_gather | solution.py:19
  304.4 215.2 %while.10 = (s32[]{:T(128)}, f32[20,1024,256]{2,1,0:T(8,128)}, s32[20,2]{1,0:T(8,128)S(1)}, f32[2,1024,1024]{2,1,0:T(8,128)}, f32[16,256,1024]{2,1,0:T(8,128)}, /*index=5*/s32[]{:T(128)}, s32[1,1]{1,0:T(1,128)}) while((s32[]{:T(128)}, f32[20,1024,256]{2,1,0:T(8,128)}, s32[20,2]{1,0:T(8,128)S(1)}, f32[2,1024,1024]{2,1,0:T(8,128)}, ...), condition=%wide.region_3.4_spmd, body=%wide.region_0.3_spmd.sunk | while | flops 3221225472 | bytes 8389849 | solution.py:29
  305.6 8.5 %conditional.2 = (f32[1,1024,256]{2,1,0:T(8,128)S(1)}) conditional(s32[]{:T(128)} %bitcast.18, () %tuple.35, (s32[1,2]{1,0:T(1,128)S(1)}, f32[2,1024,1024]{2,1,0:T(8,128)}, f32[16,256,1024]{2,1,0:T(8,128)}) %tuple.36), branch_computations={%region_1.1_spmd, %region_2.2_spmd} | conditional | flops 3221225472 | bytes 6292042 | solution.py:23
  316.3 8.5 %conditional.2 = (f32[1,1024,256]{2,1,0:T(8,128)S(1)}) conditional(s32[]{:T(128)} %bitcast.18, () %tuple.35, (s32[1,2]{1,0:T(1,128)S(1)}, f32[2,1024,1024]{2,1,0:T(8,128)}, f32[16,256,1024]{2,1,0:T(8,128)}) %tuple.36), branch_computations={%region_1.1_spmd, %region_2.2_spmd} | conditional | flops 3221225472 | bytes 6292042 | solution.py:23
  327.1 8.5 %conditional.2 = (f32[1,1024,256]{2,1,0:T(8,128)S(1)}) conditional(s32[]{:T(128)} %bitcast.18, () %tuple.35, (s32[1,2]{1,0:T(1,128)S(1)}, f32[2,1024,1024]{2,1,0:T(8,128)}, f32[16,256,1024]{2,1,0:T(8,128)}) %tuple.36), branch_computations={%region_1.1_spmd, %region_2.2_spmd} | conditional | flops 3221225472 | bytes 6292042 | solution.py:23
  337.8 8.5 %conditional.2 = (f32[1,1024,256]{2,1,0:T(8,128)S(1)}) conditional(s32[]{:T(128)} %bitcast.18, () %tuple.35, (s32[1,2]{1,0:T(1,128)S(1)}, f32[2,1024,1024]{2,1,0:T(8,128)}, f32[16,256,1024]{2,1,0:T(8,128)}) %tuple.36), branch_computations={%region_1.1_spmd, %region_2.2_spmd} | conditional | flops 3221225472 | bytes 6292042 | solution.py:23
  348.6 8.6 %conditional.2 = (f32[1,1024,256]{2,1,0:T(8,128)S(1)}) conditional(s32[]{:T(128)} %bitcast.18, () %tuple.35, (s32[1,2]{1,0:T(1,128)S(1)}, f32[2,1024,1024]{2,1,0:T(8,128)}, f32[16,256,1024]{2,1,0:T(8,128)}) %tuple.36), branch_computations={%region_1.1_spmd, %region_2.2_spmd} | conditional | flops 3221225472 | bytes 6292042 | solution.py:23
  351.6 5.6 %fusion.3 = f32[1,1024,256]{2,1,0:T(8,128)S(1)} fusion(f32[2,1024,1024]{2,1,0:T(8,128)} %get-tuple-element.31, s32[]{:T(128)S(6)} %select_n.0, f32[16,256,1024]{2,1,0:T(8,128)} %get-tuple-element.33, s32[]{:T(128)} %bitcast.2), kind=kOutput, calls=%fused_computation.3 | convolution fusion | flops 3221225472 | bytes 6291972 | tf_op jit(solution)/shard_map/while/body/eval_jaxpr/cond/branch_1_fun/ak,bk->ab/dot_general | solution.py:10
  359.4 8.5 %conditional.2 = (f32[1,1024,256]{2,1,0:T(8,128)S(1)}) conditional(s32[]{:T(128)} %bitcast.18, () %tuple.35, (s32[1,2]{1,0:T(1,128)S(1)}, f32[2,1024,1024]{2,1,0:T(8,128)}, f32[16,256,1024]{2,1,0:T(8,128)}) %tuple.36), branch_computations={%region_1.1_spmd, %region_2.2_spmd} | conditional | flops 3221225472 | bytes 6292042 | solution.py:23
  370.1 8.6 %conditional.2 = (f32[1,1024,256]{2,1,0:T(8,128)S(1)}) conditional(s32[]{:T(128)} %bitcast.18, () %tuple.35, (s32[1,2]{1,0:T(1,128)S(1)}, f32[2,1024,1024]{2,1,0:T(8,128)}, f32[16,256,1024]{2,1,0:T(8,128)}) %tuple.36), branch_computations={%region_1.1_spmd, %region_2.2_spmd} | conditional | flops 3221225472 | bytes 6292042 | solution.py:23
  373.1 5.6 %fusion.3 = f32[1,1024,256]{2,1,0:T(8,128)S(1)} fusion(f32[2,1024,1024]{2,1,0:T(8,128)} %get-tuple-element.31, s32[]{:T(128)S(6)} %select_n.0, f32[16,256,1024]{2,1,0:T(8,128)} %get-tuple-element.33, s32[]{:T(128)} %bitcast.2), kind=kOutput, calls=%fused_computation.3 | convolution fusion | flops 3221225472 | bytes 6291972 | tf_op jit(solution)/shard_map/while/body/eval_jaxpr/cond/branch_1_fun/ak,bk->ab/dot_general | solution.py:10
  380.9 8.5 %conditional.2 = (f32[1,1024,256]{2,1,0:T(8,128)S(1)}) conditional(s32[]{:T(128)} %bitcast.18, () %tuple.35, (s32[1,2]{1,0:T(1,128)S(1)}, f32[2,1024,1024]{2,1,0:T(8,128)}, f32[16,256,1024]{2,1,0:T(8,128)}) %tuple.36), branch_computations={%region_1.1_spmd, %region_2.2_spmd} | conditional | flops 3221225472 | bytes 6292042 | solution.py:23
  391.6 8.6 %conditional.2 = (f32[1,1024,256]{2,1,0:T(8,128)S(1)}) conditional(s32[]{:T(128)} %bitcast.18, () %tuple.35, (s32[1,2]{1,0:T(1,128)S(1)}, f32[2,1024,1024]{2,1,0:T(8,128)}, f32[16,256,1024]{2,1,0:T(8,128)}) %tuple.36), branch_computations={%region_1.1_spmd, %region_2.2_spmd} | conditional | flops 3221225472 | bytes 6292042 | solution.py:23
  394.6 5.6 %fusion.3 = f32[1,1024,256]{2,1,0:T(8,128)S(1)} fusion(f32[2,1024,1024]{2,1,0:T(8,128)} %get-tuple-element.31, s32[]{:T(128)S(6)} %select_n.0, f32[16,256,1024]{2,1,0:T(8,128)} %get-tuple-element.33, s32[]{:T(128)} %bitcast.2), kind=kOutput, calls=%fused_computation.3 | convolution fusion | flops 3221225472 | bytes 6291972 | tf_op jit(solution)/shard_map/while/body/eval_jaxpr/cond/branch_1_fun/ak,bk->ab/dot_general | solution.py:10
  402.4 8.5 %conditional.2 = (f32[1,1024,256]{2,1,0:T(8,128)S(1)}) conditional(s32[]{:T(128)} %bitcast.18, () %tuple.35, (s32[1,2]{1,0:T(1,128)S(1)}, f32[2,1024,1024]{2,1,0:T(8,128)}, f32[16,256,1024]{2,1,0:T(8,128)}) %tuple.36), branch_computations={%region_1.1_spmd, %region_2.2_spmd} | conditional | flops 3221225472 | bytes 6292042 | solution.py:23
  413.2 8.6 %conditional.2 = (f32[1,1024,256]{2,1,0:T(8,128)S(1)}) conditional(s32[]{:T(128)} %bitcast.18, () %tuple.35, (s32[1,2]{1,0:T(1,128)S(1)}, f32[2,1024,1024]{2,1,0:T(8,128)}, f32[16,256,1024]{2,1,0:T(8,128)}) %tuple.36), branch_computations={%region_1.1_spmd, %region_2.2_spmd} | conditional | flops 3221225472 | bytes 6292042 | solution.py:23
  416.1 5.6 %fusion.3 = f32[1,1024,256]{2,1,0:T(8,128)S(1)} fusion(f32[2,1024,1024]{2,1,0:T(8,128)} %get-tuple-element.31, s32[]{:T(128)S(6)} %select_n.0, f32[16,256,1024]{2,1,0:T(8,128)} %get-tuple-element.33, s32[]{:T(128)} %bitcast.2), kind=kOutput, calls=%fused_computation.3 | convolution fusion | flops 3221225472 | bytes 6291972 | tf_op jit(solution)/shard_map/while/body/eval_jaxpr/cond/branch_1_fun/ak,bk->ab/dot_general | solution.py:10
  423.9 8.5 %conditional.2 = (f32[1,1024,256]{2,1,0:T(8,128)S(1)}) conditional(s32[]{:T(128)} %bitcast.18, () %tuple.35, (s32[1,2]{1,0:T(1,128)S(1)}, f32[2,1024,1024]{2,1,0:T(8,128)}, f32[16,256,1024]{2,1,0:T(8,128)}) %tuple.36), branch_computations={%region_1.1_spmd, %region_2.2_spmd} | conditional | flops 3221225472 | bytes 6292042 | solution.py:23
  434.7 8.6 %conditional.2 = (f32[1,1024,256]{2,1,0:T(8,128)S(1)}) conditional(s32[]{:T(128)} %bitcast.18, () %tuple.35, (s32[1,2]{1,0:T(1,128)S(1)}, f32[2,1024,1024]{2,1,0:T(8,128)}, f32[16,256,1024]{2,1,0:T(8,128)}) %tuple.36), branch_computations={%region_1.1_spmd, %region_2.2_spmd} | conditional | flops 3221225472 | bytes 6292042 | solution.py:23
  437.6 5.6 %fusion.3 = f32[1,1024,256]{2,1,0:T(8,128)S(1)} fusion(f32[2,1024,1024]{2,1,0:T(8,128)} %get-tuple-element.31, s32[]{:T(128)S(6)} %select_n.0, f32[16,256,1024]{2,1,0:T(8,128)} %get-tuple-element.33, s32[]{:T(128)} %bitcast.2), kind=kOutput, calls=%fused_computation.3 | convolution fusion | flops 3221225472 | bytes 6291972 | tf_op jit(solution)/shard_map/while/body/eval_jaxpr/cond/branch_1_fun/ak,bk->ab/dot_general | solution.py:10
  445.4 8.5 %conditional.2 = (f32[1,1024,256]{2,1,0:T(8,128)S(1)}) conditional(s32[]{:T(128)} %bitcast.18, () %tuple.35, (s32[1,2]{1,0:T(1,128)S(1)}, f32[2,1024,1024]{2,1,0:T(8,128)}, f32[16,256,1024]{2,1,0:T(8,128)}) %tuple.36), branch_computations={%region_1.1_spmd, %region_2.2_spmd} | conditional | flops 3221225472 | bytes 6292042 | solution.py:23
  456.2 8.6 %conditional.2 = (f32[1,1024,256]{2,1,0:T(8,128)S(1)}) conditional(s32[]{:T(128)} %bitcast.18, () %tuple.35, (s32[1,2]{1,0:T(1,128)S(1)}, f32[2,1024,1024]{2,1,0:T(8,128)}, f32[16,256,1024]{2,1,0:T(8,128)}) %tuple.36), branch_computations={%region_1.1_spmd, %region_2.2_spmd} | conditional | flops 3221225472 | bytes 6292042 | solution.py:23
  459.2 5.6 %fusion.3 = f32[1,1024,256]{2,1,0:T(8,128)S(1)} fusion(f32[2,1024,1024]{2,1,0:T(8,128)} %get-tuple-element.31, s32[]{:T(128)S(6)} %select_n.0, f32[16,256,1024]{2,1,0:T(8,128)} %get-tuple-element.33, s32[]{:T(128)} %bitcast.2), kind=kOutput, calls=%fused_computation.3 | convolution fusion | flops 3221225472 | bytes 6291972 | tf_op jit(solution)/shard_map/while/body/eval_jaxpr/cond/branch_1_fun/ak,bk->ab/dot_general | solution.py:10
  466.9 8.5 %conditional.2 = (f32[1,1024,256]{2,1,0:T(8,128)S(1)}) conditional(s32[]{:T(128)} %bitcast.18, () %tuple.35, (s32[1,2]{1,0:T(1,128)S(1)}, f32[2,1024,1024]{2,1,0:T(8,128)}, f32[16,256,1024]{2,1,0:T(8,128)}) %tuple.36), branch_computations={%region_1.1_spmd, %region_2.2_spmd} | conditional | flops 3221225472 | bytes 6292042 | solution.py:23
  477.7 8.6 %conditional.2 = (f32[1,1024,256]{2,1,0:T(8,128)S(1)}) conditional(s32[]{:T(128)} %bitcast.18, () %tuple.35, (s32[1,2]{1,0:T(1,128)S(1)}, f32[2,1024,1024]{2,1,0:T(8,128)}, f32[16,256,1024]{2,1,0:T(8,128)}) %tuple.36), branch_computations={%region_1.1_spmd, %region_2.2_spmd} | conditional | flops 3221225472 | bytes 6292042 | solution.py:23
  488.5 8.5 %conditional.2 = (f32[1,1024,256]{2,1,0:T(8,128)S(1)}) conditional(s32[]{:T(128)} %bitcast.18, () %tuple.35, (s32[1,2]{1,0:T(1,128)S(1)}, f32[2,1024,1024]{2,1,0:T(8,128)}, f32[16,256,1024]{2,1,0:T(8,128)}) %tuple.36), branch_computations={%region_1.1_spmd, %region_2.2_spmd} | conditional | flops 3221225472 | bytes 6292042 | solution.py:23
  499.2 8.6 %conditional.2 = (f32[1,1024,256]{2,1,0:T(8,128)S(1)}) conditional(s32[]{:T(128)} %bitcast.18, () %tuple.35, (s32[1,2]{1,0:T(1,128)S(1)}, f32[2,1024,1024]{2,1,0:T(8,128)}, f32[16,256,1024]{2,1,0:T(8,128)}) %tuple.36), branch_computations={%region_1.1_spmd, %region_2.2_spmd} | conditional | flops 3221225472 | bytes 6292042 | solution.py:23
  510.0 8.5 %conditional.2 = (f32[1,1024,256]{2,1,0:T(8,128)S(1)}) conditional(s32[]{:T(128)} %bitcast.18, () %tuple.35, (s32[1,2]{1,0:T(1,128)S(1)}, f32[2,1024,1024]{2,1,0:T(8,128)}, f32[16,256,1024]{2,1,0:T(8,128)}) %tuple.36), branch_computations={%region_1.1_spmd, %region_2.2_spmd} | conditional | flops 3221225472 | bytes 6292042 | solution.py:23
  519.6 21.9 %sub.3 = f32[20,1024,256]{2,1,0:T(8,128)} subtract(f32[20,1024,256]{2,1,0:T(8,128)} %param.10, f32[20,1024,256]{2,1,0:T(8,128)} %get-tuple-element.43) | non-fusion elementwise | flops 5242880 | bytes 62914560 | tf_op jit(solution)/shard_map/sub | solution.py:30
  (108 shorter events, 124.3 us)
Async XLA Ops:
  7.2 48.5 %copy-start = (f32[2,256,1024]{2,1,0:T(8,128)S(1)}, f32[2,256,1024]{2,1,0:T(8,128)}, u32[]{:S(2)}) copy-start(f32[2,256,1024]{2,1,0:T(8,128)} %param.9) | copy-start | bytes 6291460
  7.2 58.9 %copy-start.2 = (s32[20,2]{0,1:T(2,128)S(1)}, s32[20,2]{0,1:T(2,128)}, u32[]{:S(2)}) copy-start(s32[20,2]{0,1:T(2,128)} %param.11) | copy-start | bytes 484
  7.2 48.5 %all-gather.4.cloned.1.call-start = ((), (), s32[]{:S(2)}) async-start(), calls=%async_computation | async-start | bytes 4718592 | tf_op jit(solution)/shard_map/all_gather | solution.py:14
  7.9 145.5 %all-gather.6.cloned.1.call-start = ((), (), s32[]{:S(2)}) async-start(), calls=%async_computation.1 | async-start | bytes 10485760 | tf_op jit(solution)/shard_map/all_gather | solution.py:18
  65.3 239.1 %all-gather.8.cloned.1.call-start = ((), (), s32[]{:S(2)}) async-start(), calls=%async_computation.2 | async-start | bytes 18874368 | tf_op jit(solution)/shard_map/all_gather | solution.py:19
  519.6 21.9 %copy-start.1 = (f32[2,256,1024]{2,1,0:T(8,128)S(1)}, f32[2,256,1024]{2,1,0:T(8,128)}, u32[]{:S(2)}) copy-start(f32[2,256,1024]{2,1,0:T(8,128)} %param.9) | copy-start | bytes 6291460
Sparse Core Ops, SparseCore 0:
  9.6 46.0 all-gather.3
  65.5 87.8 all-gather.5
  155.6 148.8 all-gather.7
where the time goes:
time: 550 us; the launch traced here: 548 us
  waiting for transfers between devices  287 us (52%)
  matrix products  121 us (22%)
  loops' own time  59 us (11%)
  local copies, waits for them, and re-layouts  44.7 us (8%)
  other arithmetic  21.9 us (4%)
  between operations  13.8 us (3%)
    all_gather x1, waiting for transfers between devices, per_device(): slices = lax.all_gather(solved, 'row', axis=0, tiled=True)  151 us
    dot_general x20, matrix products, slot_term(): return jnp.einsum('ak,bk->ab', left_tile, right_rows, precision=highest)  112 us
    all_gather x1, waiting for transfers between devices, per_device(): whole_tiles = lax.all_gather(solved, 'col', axis=1, tiled=True)  87.2 us
    all_gather x1, waiting for transfers between devices, per_device(): full_pivot = lax.all_gather(pivot_inverse, 'row', axis=0, tiled=True)  47.7 us
    another operation x20, loops' own time, owner_slot(): lax.cond(listed[1] >= 0, lambda: slot_term(whole_tiles[listed[0]], slices...  47.3 us
    sub x1, other arithmetic, per_device(): return (solved, trailing - updates)  21.9 us
    dynamic_update_slice x20, local copies, waits for them, and re-layouts, per_device(): updates = lax.map(owner_slot, tile_list)  20.9 us
    slice x20, local copies, waits for them, and re-layouts, owner_slot(): listed[1]  12.1 us
  transfers between devices with their start and end apart: 3, of which 3 were waited for; matrix products, arithmetic and copies ran while one was open for 0% of the time, Pallas kernels for 0%

commit v1 on v0

v1 whole, which is shorter than its diff:
```python
import functools

import jax
import jax.numpy as jnp
from jax import lax
from jax.experimental import pallas as pl
from jax.experimental.pallas import tpu as pltpu
from jax.sharding import PartitionSpec as P

MESH = pl.DeviceIdType.MESH
LIGHT = 6
CHUNKS = 4
f32, bf16 = jnp.float32, jnp.bfloat16


def halves(x):
    hi = x.astype(bf16)
    return hi, (x - hi.astype(f32)).astype(bf16)


def dot_nt(a, b):
    return lax.dot_general(a, b, (((1,), (1,)), ((), ())), preferred_element_type=f32)


def dot_nn(a, b):
    return lax.dot_general(a, b, (((1,), (0,)), ((), ())), preferred_element_type=f32)


def table(index, values):
    found = jnp.int32(0)
    for at, value in enumerate(values):
        found = jnp.where(index == at, jnp.int32(value), found)
    return found


def kernel(rows, cols, pivot, panel, trailing, tiles, solved, updated,
           sl, q, factor, own_hi, own_lo, solved_buf, q3, acc,
           load_sem, in_sem, out_sem, solved_sem,
           lz_recv, lz_send, lr_recv, lr_send, ls_recv, ls_send,
           row_recv, row_send, sib_recv, sib_send, q_recv, q_send):
    chips = rows // 2
    pan, height, order = panel.shape
    slots = trailing.shape[0]
    kc = order // CHUNKS
    far = cols // 2
    rest = 3 if chips > 3 else chips
    ring = [i ^ (i >> 1) for i in range(cols)]
    where_in = [ring.index(i) for i in range(cols)]

    row, col = lax.axis_index("row"), lax.axis_index("col")
    chip, core = lax.div(row, 2), lax.rem(row, 2)
    spot = table(col, where_in)

    def ring_col(step):
        return table(lax.rem(spot + step + cols, cols), ring)

    above, below = (row + 2, col), (row - 2, col)
    sibling = (chip * 2 + 1 - core, col)
    ahead, behind = (row, ring_col(1)), (row, ring_col(-1))
    has_above, has_below = chip < chips - 1, chip > 0
    live = jnp.where(row < rows // 2, jnp.int32(min(LIGHT, slots)), jnp.int32(slots))

    def own_panel(c):
        return pltpu.make_async_copy(
            panel.at[:, :, pl.ds(c * kc, kc)], sl[c].at[pl.ds(row * pan, pan)], load_sem.at[c])

    share = pivot.shape[0] // cols
    own_factor = pltpu.make_async_copy(
        pivot.at[pl.ds(pl.multiple_of(col * share, share), share)], factor.at[core, col, chip], load_sem.at[CHUNKS])
    own_factor.start()
    for c in range(CHUNKS):
        own_panel(c).start()

    def slot_in(t):
        return pltpu.make_async_copy(trailing.at[t], acc.at[t], in_sem.at[t])

    def slot_out(t):
        return pltpu.make_async_copy(acc.at[t], updated.at[t], out_sem.at[t])

    def slot_pass(t):
        return pltpu.make_async_copy(trailing.at[t], updated.at[t], out_sem.at[t])

    def over(lo, hi, act):
        def body(t, carry):
            act(t)
            return carry
        lax.fori_loop(lo, hi, body, 0)

    barrier = pltpu.get_barrier_semaphore()
    for other in (sibling, ahead, behind):
        pl.semaphore_signal(barrier, inc=1, device_id=other, device_id_type=MESH)

    @pl.when(has_above)
    def _():
        pl.semaphore_signal(barrier, inc=1, device_id=above, device_id_type=MESH)

    @pl.when(has_below)
    def _():
        pl.semaphore_signal(barrier, inc=1, device_id=below, device_id_type=MESH)

    pl.semaphore_wait(barrier, 3 + jnp.where(has_above, 1, 0) + jnp.where(has_below, 1, 0))

    def remote(ref, send, recv, device):
        return pltpu.make_async_remote_copy(
            src_ref=ref, dst_ref=ref, send_sem=send, recv_sem=recv, device_id=device, device_id_type=MESH)

    def factor_line(up, src):
        return remote(factor.at[core, col, src], lz_send.at[0 if up else 1, src], lz_recv.at[src], above if up else below)

    hc = chips // 2

    def factor_part(side, at, h):
        return factor.at[side, at, pl.ds(h * hc, hc)]

    def factor_ring(fwd, at, h):
        return remote(factor_part(core, at, h), lr_send.at[0 if fwd else 1, at, h], lr_recv.at[at, h], ahead if fwd else behind)

    def factor_sib(side, at, h):
        return remote(factor_part(side, at, h), ls_send.at[at, h], ls_recv.at[at, h], sibling)

    def slices_of(c, src, side):
        return sl[c].at[pl.ds((src * 2 + side) * pan, pan)]

    def row_line(c, up, src):
        return remote(slices_of(c, src, core), row_send.at[c, 0 if up else 1, src], row_recv.at[c, src], above if up else below)

    def row_sib(c, src, side):
        return remote(slices_of(c, src, side), sib_send.at[c, src], sib_recv.at[c, src], sibling)

    def q_ring(c, fwd, at, h):
        return remote(q[c].at[h, at], q_send.at[c, 0 if fwd else 1, at, h], q_recv.at[c, at, h], ahead if fwd else behind)

    def line_own(make):
        @pl.when(has_above)
        def _():
            make(True, chip).start()

        @pl.when(has_below)
        def _():
            make(False, chip).start()

    def line_event(make, d, also):
        @pl.when(chip - d >= 0)
        def _():
            make(True, chip - d).wait_recv()

            @pl.when(has_above)
            def _():
                make(True, chip - d).start()
            also(chip - d)

        @pl.when(chip + d < chips)
        def _():
            make(False, chip + d).wait_recv()

            @pl.when(has_below)
            def _():
                make(False, chip + d).start()
            also(chip + d)

    def line_drain(make):
        @pl.when(has_above)
        def _():
            over(0, chip + 1, lambda src: make(True, src).wait_send())

        @pl.when(has_below)
        def _():
            over(chip, chips, lambda src: make(False, src).wait_send())

    def goes(d, fwd, h, count):
        return d < far or (d == far and (2 * h < count) == fwd)

    def ring_event(make, d, count, also):
        for h in range(count):
            for fwd in (True, False):
                if goes(d, fwd, h, count):
                    at = ring_col(-d if fwd else d)
                    if d > 0:
                        make(fwd, at, h).wait_recv()
                    if goes(d + 1, fwd, h, count):
                        make(fwd, at, h).start()
                    if d > 0:
                        also(at, h)

    def ring_drain(make, count):
        for d in range(far):
            for h in range(count):
                for fwd in (True, False):
                    if goes(d + 1, fwd, h, count):
                        make(fwd, ring_col(-d if fwd else d), h).wait_send()

    def row_own(c):
        line_own(functools.partial(row_line, c))
        row_sib(c, chip, core).start()

    def row_event(c, lo, hi):
        for d in range(lo, hi):
            line_event(functools.partial(row_line, c), d, lambda src: row_sib(c, src, core).start())

    def q_event(c, d):
        ring_event(functools.partial(q_ring, c), d, pan, lambda at, h: None)

    own_factor.wait()
    line_own(factor_line)
    own_panel(0).wait()
    row_own(0)
    over(0, live, lambda t: slot_in(t).start())
    over(live, slots, lambda t: slot_pass(t).start())
    for c in range(1, CHUNKS):
        own_panel(c).wait()

    for c in range(CHUNKS):
        hi, lo = halves(sl[c][pl.ds(row * pan, pan)].reshape(pan * height, kc))
        own_hi[:, c * kc:(c + 1) * kc] = hi
        own_lo[:, c * kc:(c + 1) * kc] = lo

    for d in range(1, chips):
        line_event(factor_line, d, lambda src: None)
    row_own(1)

    def pass_factor(at, h):
        factor_sib(core, at, h).start()

    ring_event(factor_ring, 0, 2, pass_factor)
    for h in range(2):
        pass_factor(col, h)
    row_event(0, 1, 2)
    ring_event(factor_ring, 1, 2, pass_factor)
    row_event(0, 2, rest)
    for d in range(2, far + 1):
        ring_event(factor_ring, d, 2, pass_factor)
    row_own(2)
    for at in range(cols):
        for h in range(2):
            factor_sib(1 - core, at, h).wait_recv()
    row_event(1, 1, 2)

    block = order // chips
    for b in range(chips):
        depth = min(order, -(-((b + 1) * block) // 128) * 128)
        l_hi, l_lo = halves(factor[:, :, b, :, :depth].reshape(block, depth))
        a_hi, a_lo = own_hi[:, :depth], own_lo[:, :depth]
        part = dot_nt(a_hi, l_hi) + (dot_nt(a_hi, l_lo) + dot_nt(a_lo, l_hi))
        solved_buf[:, :, b * block:(b + 1) * block] = part.reshape(pan, height, block)
    solved_copy = pltpu.make_async_copy(solved_buf, solved, solved_sem)
    for b in range(CHUNKS):
        hi, lo = halves(solved_buf[:, :, b * kc:(b + 1) * kc].reshape(pan * height, kc))
        own_hi[:, b * kc:(b + 1) * kc] = hi
        own_lo[:, b * kc:(b + 1) * kc] = lo
    solved_copy.start()

    for c in range(CHUNKS):
        first = (c * kc) // block
        span = pl.ds(c * kc, kc)
        l_rows = jnp.concatenate([factor[:, :, b, :, span].reshape(block, kc) for b in range(first, chips)], axis=0)
        l_hi, l_lo = halves(l_rows)
        s_hi, s_lo = own_hi[:, first * block:], own_lo[:, first * block:]
        part = dot_nn(s_hi, l_hi) + (dot_nn(s_hi, l_lo) + dot_nn(s_lo, l_hi))
        part = part.reshape(pan, height, kc)
        for h in range(pan):
            q[c][h, col] = part[h]
        q_event(c, 0)
        if c == 1:
            row_event(1, 2, rest)
    row_own(3)
    q_event(0, 1)

    def update(c, part, parts):
        def one(t):
            left = q3[tiles[t, 0]]
            r_hi, r_lo = halves(sl[c][tiles[t, 1]])
            right = jnp.concatenate([r_hi, r_lo, r_hi], axis=1)
            if c == 0:
                slot_in(t).wait()
            acc[t] = acc[t] - dot_nt(left, right)
            if c == CHUNKS - 1:
                slot_out(t).start()
        over(live * part // parts, live * (part + 1) // parts, one)

    for c in range(CHUNKS):
        for d in range(2, far + 1):
            q_event(c, d)
        if c + 1 < CHUNKS:
            q_event(c + 1, 1)
        for h in range(pan):
            hi, lo = halves(q[c][h].reshape(cols * height, kc))
            q3[h, :, 0:kc] = hi
            q3[h, :, kc:2 * kc] = hi
            q3[h, :, 2 * kc:3 * kc] = lo
        row_event(c, rest, chips)
        over(0, chips, lambda src: row_sib(c, src, 1 - core).wait_recv())
        update(c, 0, 2)
        if c + 2 < CHUNKS:
            row_event(c + 2, 1, 2)
        update(c, 1, 2)
        if c + 2 < CHUNKS:
            row_event(c + 2, 2, rest)

    line_drain(factor_line)
    ring_drain(factor_ring, 2)
    for at in range(cols):
        for h in range(2):
            factor_sib(core, at, h).wait_send()
    for c in range(CHUNKS):
        line_drain(functools.partial(row_line, c))
        over(0, chips, lambda src: row_sib(c, src, core).wait_send())
        ring_drain(functools.partial(q_ring, c), pan)
    solved_copy.wait()
    over(0, live, lambda t: slot_out(t).wait())
    over(live, slots, lambda t: slot_pass(t).wait())


def per_device(rows, cols, pivot_inverse, panel, trailing, tile_list):
    pan, height, order = panel.shape
    slots, _, width = trailing.shape
    chips, kc = rows // 2, order // CHUNKS
    share = pivot_inverse.shape[0] // cols
    dma = pltpu.SemaphoreType.DMA
    anywhere = pl.BlockSpec(memory_space=pltpu.HBM)
    return pl.pallas_call(
        functools.partial(kernel, rows, cols),
        out_shape=(
            jax.ShapeDtypeStruct(panel.shape, f32),
            jax.ShapeDtypeStruct(trailing.shape, f32),
        ),
        in_specs=[anywhere, anywhere, anywhere, pl.BlockSpec(memory_space=pltpu.SMEM)],
        out_specs=(anywhere, anywhere),
        scratch_shapes=[
            [pltpu.VMEM((rows * pan, height, kc), f32) for _ in range(CHUNKS)],
            [pltpu.VMEM((pan, cols, height, kc), f32) for _ in range(CHUNKS)],
            pltpu.VMEM((2, cols, chips, share, order), f32),
            pltpu.VMEM((pan * height, order), bf16),
            pltpu.VMEM((pan * height, order), bf16),
            pltpu.VMEM((pan, height, order), f32),
            pltpu.VMEM((pan, cols * height, 3 * kc), bf16),
            pltpu.VMEM((slots, order, width), f32),
            dma((CHUNKS + 1,)),
            dma((slots,)),
            dma((slots,)),
            dma(()),
            dma((chips,)),
            dma((2, chips)),
            dma((cols, 2)),
            dma((2, cols, 2)),
            dma((cols, 2)),
            dma((cols, 2)),
            dma((CHUNKS, chips)),
            dma((CHUNKS, 2, chips)),
            dma((CHUNKS, chips)),
            dma((CHUNKS, chips)),
            dma((CHUNKS, cols, pan)),
            dma((CHUNKS, 2, cols, pan)),
        ],
        compiler_params=pltpu.CompilerParams(
            collective_id=0, has_side_effects=True, vmem_limit_bytes=67043328
        ),
    )(pivot_inverse, panel, trailing, tile_list)


def solution(mesh):
    placed = (P("row", None), P("row", "col", None), P("row", None, "col"), P("row", None))
    return jax.shard_map(
        functools.partial(per_device, mesh.shape["row"], mesh.shape["col"]),
        mesh=mesh,
        in_specs=placed,
        out_specs=(P("row", "col", None), P("row", None, "col")),
        check_vma=False,
    )
```

time: 550 us -> 473 us (0.86)
  the two profiles are of different devices: /device:TPU:27 before, /device:TPU:0 now
where the time goes in v1:
time: 473 us
  Pallas kernels  452 us (96%)
  local copies, waits for them, and re-layouts  20.3 us (4%)
    pallas_call x1, Pallas kernels, per_device(): pl.pallas_call(functools.partial(kernel, rows, cols), out_shape=(jax.Shap...  452 us
    unnamed x3, local copies, waits for them, and re-layouts  20.3 us

profile of v1, /device:TPU:0, one launch (start us, length us, event | category | flops | bytes accessed | tf_op | source)
XLA Modules:
  0.0 473.2 jit_solution(7171297876433189290)
XLA Ops:
  0.6 1.4 copy.6.tiles
  2.0 452.2 %shard_map.59 = (f32[2,256,1024]{2,1,0:T(8,128)}, f32[20,1024,256]{2,1,0:T(8,128)}) custom-call(f32[128,1024]{1,0:T(8,128)} %pivot.1, f32[2,256,1024]{2,1,0:T(8,128)} %panel.1, f32[20,1024,256]{2,1,0:T(8,128)} %trailing.1, s32[20,2]{1,0:T(8,128)} %copy.6.tiles), custom_call_target="tpu_custom_call" | custom-call | tf_op jit(solution)/shard_map/pallas_call | solution.py:320
  454.2 3.2 copy.9
  457.4 15.8 %copy.10 = f32[20,1024,256]{2,1,0:T(8,128)} copy(f32[20,1024,256]{2,1,0:T(8,128)} %get-tuple-element.5) | data formatting | bytes 41943040

commit v2 on v1

--- a/solution.py
+++ b/solution.py
@@ -77,9 +77,6 @@
     def slot_out(t):
         return pltpu.make_async_copy(acc.at[t], updated.at[t], out_sem.at[t])
 
-    def slot_pass(t):
-        return pltpu.make_async_copy(trailing.at[t], updated.at[t], out_sem.at[t])
-
     def over(lo, hi, act):
         def body(t, carry):
             act(t)
@@ -204,8 +201,7 @@
     line_own(factor_line)
     own_panel(0).wait()
     row_own(0)
-    over(0, live, lambda t: slot_in(t).start())
-    over(live, slots, lambda t: slot_pass(t).start())
+    over(0, slots, lambda t: slot_in(t).start())
     for c in range(1, CHUNKS):
         own_panel(c).wait()
 
@@ -217,6 +213,12 @@
     for d in range(1, chips):
         line_event(factor_line, d, lambda src: None)
     row_own(1)
+
+    def untouched(t):
+        slot_in(t).wait()
+        slot_out(t).start()
+
+    over(live, slots, untouched)
 
     def pass_factor(at, h):
         factor_sib(core, at, h).start()
@@ -306,8 +308,7 @@
         over(0, chips, lambda src: row_sib(c, src, core).wait_send())
         ring_drain(functools.partial(q_ring, c), pan)
     solved_copy.wait()
-    over(0, live, lambda t: slot_out(t).wait())
-    over(live, slots, lambda t: slot_pass(t).wait())
+    over(0, slots, lambda t: slot_out(t).wait())
 
 
 def per_device(rows, cols, pivot_inverse, panel, trailing, tile_list):
@@ -316,7 +317,7 @@
     chips, kc = rows // 2, order // CHUNKS
     share = pivot_inverse.shape[0] // cols
     dma = pltpu.SemaphoreType.DMA
-    anywhere = pl.BlockSpec(memory_space=pltpu.HBM)
+    anywhere = pl.BlockSpec(memory_space=pl.ANY)
     return pl.pallas_call(
         functools.partial(kernel, rows, cols),
         out_shape=(

time: 473 us -> 199 us (0.42)
  the two profiles are of different devices: /device:TPU:0 before, /device:TPU:27 now
where the time goes in v2:
time: 199 us
  Pallas kernels  178 us (89%)
  local copies, waits for them, and re-layouts  20.3 us (10%)
    pallas_call x1, Pallas kernels, per_device(): pl.pallas_call(functools.partial(kernel, rows, cols), out_shape=(jax.Shap...  178 us
    unnamed x3, local copies, waits for them, and re-layouts  20.3 us

profile of v2, /device:TPU:27, one launch (start us, length us, event | category | flops | bytes accessed | tf_op | source)
XLA Modules:
  0.0 198.7 jit_solution(1098380090137165582)
XLA Ops:
  0.6 1.4 copy.6.tiles
  2.0 177.8 %shard_map.59 = (f32[2,256,1024]{2,1,0:T(8,128)}, f32[20,1024,256]{2,1,0:T(8,128)}) custom-call(f32[128,1024]{1,0:T(8,128)} %pivot.1, f32[2,256,1024]{2,1,0:T(8,128)} %panel.1, f32[20,1024,256]{2,1,0:T(8,128)} %trailing.1, s32[20,2]{1,0:T(8,128)} %copy.6.tiles), custom_call_target="tpu_custom_call" | custom-call | tf_op jit(solution)/shard_map/pallas_call | solution.py:321
  179.8 3.2 %copy.9 = f32[2,256,1024]{2,1,0:T(8,128)} copy(f32[2,256,1024]{2,1,0:T(8,128)} %get-tuple-element.4) | data formatting | bytes 4194304
  182.9 15.8 %copy.10 = f32[20,1024,256]{2,1,0:T(8,128)} copy(f32[20,1024,256]{2,1,0:T(8,128)} %get-tuple-element.5) | data formatting | bytes 41943040

commit v3 on v2

--- a/solution.py
+++ b/solution.py
@@ -33,9 +33,9 @@
     return found
 
 
-def kernel(rows, cols, pivot, panel, trailing, tiles, solved, updated,
+def kernel(rows, cols, pivot, panel, trailing, tiles, solved, updated, last_slices, last_left,
            sl, q, factor, own_hi, own_lo, solved_buf, q3, acc,
-           load_sem, in_sem, out_sem, solved_sem,
+           load_sem, in_sem, out_sem, solved_sem, last_sem,
            lz_recv, lz_send, lr_recv, lr_send, ls_recv, ls_send,
            row_recv, row_send, sib_recv, sib_send, q_recv, q_send):
     chips = rows // 2
@@ -275,7 +275,7 @@
             if c == 0:
                 slot_in(t).wait()
             acc[t] = acc[t] - dot_nt(left, right)
-            if c == CHUNKS - 1:
+            if c == CHUNKS - 2:
                 slot_out(t).start()
         over(live * part // parts, live * (part + 1) // parts, one)
 
@@ -291,12 +291,19 @@
             q3[h, :, 2 * kc:3 * kc] = lo
         row_event(c, rest, chips)
         over(0, chips, lambda src: row_sib(c, src, 1 - core).wait_recv())
+        if c == CHUNKS - 1:
+            break
         update(c, 0, 2)
         if c + 2 < CHUNKS:
             row_event(c + 2, 1, 2)
         update(c, 1, 2)
         if c + 2 < CHUNKS:
             row_event(c + 2, 2, rest)
+
+    keep = (pltpu.make_async_copy(sl[CHUNKS - 1], last_slices, last_sem.at[0]),
+            pltpu.make_async_copy(q3, last_left, last_sem.at[1]))
+    for copy in keep:
+        copy.start()
 
     line_drain(factor_line)
     ring_drain(factor_ring, 2)
@@ -308,7 +315,23 @@
         over(0, chips, lambda src: row_sib(c, src, core).wait_send())
         ring_drain(functools.partial(q_ring, c), pan)
     solved_copy.wait()
+    for copy in keep:
+        copy.wait()
     over(0, slots, lambda t: slot_out(t).wait())
+
+
+def closing(tiles, partial, slices, lefts, out):
+    t = pl.program_id(0)
+
+    @pl.when(tiles[t, 1] >= 0)
+    def _():
+        r_hi, r_lo = halves(slices[tiles[t, 1]])
+        right = jnp.concatenate([r_hi, r_lo, r_hi], axis=1)
+        out[0] = partial[0] - dot_nt(lefts[tiles[t, 0]], right)
+
+    @pl.when(tiles[t, 1] < 0)
+    def _():
+        out[...] = partial[...]
 
 
 def per_device(rows, cols, pivot_inverse, panel, trailing, tile_list):
@@ -318,14 +341,16 @@
     share = pivot_inverse.shape[0] // cols
     dma = pltpu.SemaphoreType.DMA
     anywhere = pl.BlockSpec(memory_space=pl.ANY)
-    return pl.pallas_call(
+    solved, partial, last_slices, last_left = pl.pallas_call(
         functools.partial(kernel, rows, cols),
         out_shape=(
             jax.ShapeDtypeStruct(panel.shape, f32),
             jax.ShapeDtypeStruct(trailing.shape, f32),
+            jax.ShapeDtypeStruct((rows * pan, height, kc), f32),
+            jax.ShapeDtypeStruct((pan, order, 3 * kc), bf16),
         ),
         in_specs=[anywhere, anywhere, anywhere, pl.BlockSpec(memory_space=pltpu.SMEM)],
-        out_specs=(anywhere, anywhere),
+        out_specs=(anywhere,) * 4,
         scratch_shapes=[
             [pltpu.VMEM((rows * pan, height, kc), f32) for _ in range(CHUNKS)],
             [pltpu.VMEM((pan, cols, height, kc), f32) for _ in range(CHUNKS)],
@@ -339,6 +364,7 @@
             dma((slots,)),
             dma((slots,)),
             dma(()),
+            dma((2,)),
             dma((chips,)),
             dma((2, chips)),
             dma((cols, 2)),
@@ -356,6 +382,22 @@
             collective_id=0, has_side_effects=True, vmem_limit_bytes=67043328
         ),
     )(pivot_inverse, panel, trailing, tile_list)
+    one_slot = pl.BlockSpec((1, order, width), lambda t, tiles: (t, 0, 0))
+    updated = pl.pallas_call(
+        closing,
+        out_shape=jax.ShapeDtypeStruct(trailing.shape, f32),
+        grid_spec=pltpu.PrefetchScalarGridSpec(
+            num_scalar_prefetch=1,
+            grid=(slots,),
+            in_specs=[
+                one_slot,
+                pl.BlockSpec(last_slices.shape, lambda t, tiles: (0, 0, 0)),
+                pl.BlockSpec(last_left.shape, lambda t, tiles: (0, 0, 0)),
+            ],
+            out_specs=one_slot,
+        ),
+    )(tile_list, partial, last_slices, last_left)
+    return solved, updated
 
 
 def solution(mesh):

time: 199 us -> 199 us (level)
  local copies, waits for them, and re-layouts: 20.3 us -> 2.69 us
  Pallas kernels: 178 us -> 195 us
    pallas_call x0 -> x1, Pallas kernels: none -> 27.8 us  [per_device(): pl.pallas_call(closing, out_shape=jax.ShapeDtypeStruct(trailing.shape, f3...]
    unnamed x3 -> x4, local copies, waits for them, and re-layouts: 20.3 us -> 2.69 us
    pallas_call x1, Pallas kernels: 178 us -> 168 us  [per_device(): pl.pallas_call(functools.partial(kernel, rows, cols), out_shape=(jax.Shap...]
where the time goes in v3:
time: 199 us
  Pallas kernels  195 us (98%)
  local copies, waits for them, and re-layouts  2.69 us (1%)
    pallas_call x1, Pallas kernels, per_device(): pl.pallas_call(functools.partial(kernel, rows, cols), out_shape=(jax.Shap...  168 us
    pallas_call x1, Pallas kernels, per_device(): pl.pallas_call(closing, out_shape=jax.ShapeDtypeStruct(trailing.shape, f3...  27.8 us

profile of v3, /device:TPU:27, one launch (start us, length us, event | category | flops | bytes accessed | tf_op | source)
XLA Modules:
  0.0 198.7 jit_solution(3541600033025022981)
XLA Ops:
  0.6 1.4 copy.6.tiles
  2.0 167.6 %shard_map.59 = (f32[2,256,1024]{2,1,0:T(8,128)}, f32[20,1024,256]{2,1,0:T(8,128)}, f32[16,256,256]{2,1,0:T(8,128)}, bf16[2,1024,768]{2,1,0:T(8,128)(2,1)}) custom-call(f32[128,1024]{1,0:T(8,128)} %pivot.1, f32[2,256,1024]{2,1,0:T(8,128)} %panel.1, f32[20,1024,256]{2,1,0:T(8,128)} %trailing.1, s32[20,2]{1,0:T(8,128)} %copy.6.tiles), custom_call_target="tpu_custom_call" | custom-call | tf_op jit(solution)/shard_map/pallas_call | solution.py:344
  169.6 0.0 copy-start
  169.6 27.8 %shard_map.60 = f32[20,1024,256]{2,1,0:T(8,128)} custom-call(s32[20,2]{1,0:T(8,128)} %copy.6.tiles, f32[20,1024,256]{2,1,0:T(8,128)} %get-tuple-element.7.partial, f32[16,256,256]{2,1,0:T(8,128)} %get-tuple-element.8.slices, bf16[2,1024,768]{2,1,0:T(8,128)(2,1)} %get-tuple-element.9.lefts), custom_call_target="tpu_custom_call" | custom-call | tf_op jit(solution)/shard_map/pallas_call | solution.py:386
  197.4 0.0 copy-done
  197.4 1.3 copy.9
Async XLA Ops:
  169.6 27.8 %copy-start = (f32[2,256,1024]{2,1,0:T(8,128)S(1)}, f32[2,256,1024]{2,1,0:T(8,128)}, u32[]{:S(2)}) copy-start(f32[2,256,1024]{2,1,0:T(8,128)} %get-tuple-element.12) | copy-start | bytes 6291460
